TPU v7x, 256 devices: a whole 4x4x8 slice. The times are simulated.
256 devices in a mesh: dp: 32 (over z, y_hi, core), mp: 8 (over x, y_lo).
Axes of the slice: x: 4, y: 4 (y_hi: 2, y_lo: 2; y = y_hi * 2 + y_lo), z: 8, core: 2. Of those that a mesh axis runs over, the one named last changes fastest.
Arguments:
- token_ids: int32 [128, 64], P(None, 'dp'), may hold values from 0 to 1023
- fanout: int32 [128, 16], replicated, may hold values from 1 to 16
- table_of_column: int32 [64], P('dp'), may hold values from 0 to 15
- embed_table: bfloat16 [64, 1024, 1024], P('dp', 'mp'), may hold values from -35 to 35
- start_vector: bfloat16 [1024], replicated, may hold values from -6 to 6
- gain_attn: bfloat16 [1024], replicated, may hold values from 0.25 to 1.75
- gain_mlp: bfloat16 [1024], replicated, may hold values from 0.25 to 1.75
- gain_final: bfloat16 [1024], replicated, may hold values from 0.25 to 1.75
- w_qkv: bfloat16 [1024, 3, 1024], P(None, None, 'mp'), may hold values from -8 to 8
- w_out: bfloat16 [1024, 1024], P(None, 'mp'), may hold values from -0.1875 to 0.1875
- w_gate: bfloat16 [1024, 4096], P(None, 'mp'), may hold values from -0.1875 to 0.1875
- w_up: bfloat16 [1024, 4096], P(None, 'mp'), may hold values from -0.1875 to 0.1875
- w_down: bfloat16 [1024, 4096], P(None, 'mp'), may hold values from -0.09375 to 0.09375
Outputs:
- nll: float32 [128, 64], P(None, 'dp')
- grad_table: float32 [64, 1024, 1024], P('dp', 'mp')
- grad_qkv: float32 [1024, 3, 1024], P('dp', None, 'mp')
- grad_out: float32 [1024, 1024], P('dp', 'mp')
- grad_gate: float32 [1024, 4096], P('dp', 'mp')
- grad_up: float32 [1024, 4096], P('dp', 'mp')
- grad_down: float32 [1024, 4096], P('dp', 'mp')
All inputs are finite; a program needn't handle non-finite values.
Results may differ from a plain program's by a relative error of at most 0.015.
The roundings to bfloat16 on the way count: a program that leaves them out, or rounds other values in their place, can miss the bound.
Values may be sent and summed in bfloat16 or wider, within the bound.
A program may use at most 128 MiB of HBM per device.

v0:
```python
import math
import jax
import jax.numpy as jnp
from jax import lax
from jax.sharding import PartitionSpec as P

HS = 64
TABLES = 16
EPS = 1e-05
ATTN_CAP = 50.0
LOGIT_CAP = 30.0


def gather_features(values):
    return lax.all_gather(values, "mp", axis=2, tiled=True)


def feature_sum(term):
    return lax.psum_scatter(term, "mp", scatter_dimension=2, tiled=True)


def cols_to_rows(values):
    return lax.all_to_all(values, "dp", split_axis=0, concat_axis=1, tiled=True)


def rows_to_cols(values):
    return lax.all_to_all(values, "dp", split_axis=1, concat_axis=0, tiled=True)


def rms_of(values):
    floats = values.astype(jnp.float32)
    return jnp.sqrt(jnp.mean(floats * floats, axis=-1, keepdims=True) + EPS)


def normalize(values, gain, rms):
    return (values.astype(jnp.float32) / rms * gain.astype(jnp.float32)).astype(jnp.bfloat16)


def norm_back_full(values, d_norm, gain, rms):
    floats = values.astype(jnp.float32)
    gains = gain.astype(jnp.float32)
    total = jnp.sum(gains * d_norm * floats, axis=-1, keepdims=True)
    return gains * d_norm / rms - floats * total / (floats.shape[-1] * rms * rms * rms)


def norm_back_part(values, d_norm, gain, rms, model_width):
    floats = values.astype(jnp.float32)
    gains = gain.astype(jnp.float32)
    partial_total = jnp.sum(gains * d_norm * floats, axis=-1)
    total = lax.psum(partial_total, "mp")[..., None]
    return gains * d_norm / rms - floats * total / (model_width * rms * rms * rms)


def local(
    token_ids,
    fanout,
    table_of_column,
    embed_table,
    start_vector,
    gain_attn,
    gain_mlp,
    gain_final,
    w_qkv,
    w_out,
    w_gate,
    w_up,
    w_down,
):
    fl = jnp.float32
    mp_rank = lax.axis_index("mp")
    mp_count = lax.axis_size("mp")
    model_width = embed_table.shape[2]
    vocab_part = embed_table.shape[1]
    part_width = model_width // mp_count
    head_cols = w_qkv.shape[2]
    local_heads = head_cols // HS
    row_total_count = token_ids.shape[0]

    def own_part(vector):
        return lax.dynamic_slice_in_dim(vector, mp_rank * part_width, part_width, 0)

    local_ids = token_ids - mp_rank * vocab_part
    onehot = (
        local_ids[:, :, None] == jnp.arange(vocab_part, dtype=jnp.int32)[None, None, :]
    ).astype(jnp.bfloat16)
    picked = jnp.einsum("rcv,cvd->rcd", onehot, embed_table, preferred_element_type=fl)
    emb_cols = feature_sum(picked).astype(jnp.bfloat16)
    emb_rows = cols_to_rows(emb_cols)
    rows_here = emb_rows.shape[0]
    col_count = emb_rows.shape[1]
    start_rows = jnp.broadcast_to(own_part(start_vector)[None, None, :], (rows_here, 1, part_width))
    resid_in = jnp.concatenate([start_rows, emb_rows[:, :-1]], axis=1)
    in_full = gather_features(resid_in)
    rms_attn = rms_of(in_full)
    norm_attn = normalize(in_full, gain_attn, rms_attn)
    qkv = jnp.einsum("rpd,dtx->rptx", norm_attn, w_qkv, preferred_element_type=fl).astype(
        jnp.bfloat16
    )
    queries = qkv[:, :, 0].reshape(rows_here, col_count, local_heads, HS)
    key_rows = qkv[:, :, 1].reshape(rows_here, col_count, local_heads, HS)
    value_rows = qkv[:, :, 2].reshape(rows_here, col_count, local_heads, HS)
    score_raw = jnp.einsum(
        "rqhe,rkhe->rhqk", queries, key_rows, preferred_element_type=fl
    ) / math.sqrt(HS)
    score = ATTN_CAP * jnp.tanh(score_raw / ATTN_CAP)
    col_index = jnp.arange(col_count, dtype=jnp.int32)
    causal = col_index[:, None] >= col_index[None, :]
    exp_score = jnp.where(causal, jnp.exp(score), 0.0)
    attn_prob = exp_score / jnp.sum(exp_score, axis=-1, keepdims=True)
    prob_b = attn_prob.astype(jnp.bfloat16)
    attn_heads = jnp.einsum(
        "rhqk,rkhe->rqhe", prob_b, value_rows, preferred_element_type=fl
    ).astype(jnp.bfloat16)
    attn_out = attn_heads.reshape(rows_here, col_count, head_cols)
    mixed_part = jnp.einsum("rpj,dj->rpd", attn_out, w_out, preferred_element_type=fl)
    resid_mid = (resid_in.astype(fl) + feature_sum(mixed_part)).astype(jnp.bfloat16)
    mid_full = gather_features(resid_mid)
    rms_mlp = rms_of(mid_full)
    norm_mlp = normalize(mid_full, gain_mlp, rms_mlp)
    gate_pre = jnp.einsum("rpd,df->rpf", norm_mlp, w_gate, preferred_element_type=fl)
    up_proj = jnp.einsum("rpd,df->rpf", norm_mlp, w_up, preferred_element_type=fl)
    hidden = (jax.nn.silu(gate_pre) * up_proj).astype(jnp.bfloat16)
    down_part = jnp.einsum("rpf,df->rpd", hidden, w_down, preferred_element_type=fl)
    resid_out = (resid_mid.astype(fl) + feature_sum(down_part)).astype(jnp.bfloat16)
    out_cols = rows_to_cols(resid_out)
    out_full = gather_features(out_cols)
    rms_final = rms_of(out_full)
    norm_final = normalize(out_full, gain_final, rms_final)
    width_root = math.sqrt(model_width)
    logit_raw = (
        jnp.einsum("rcd,cvd->rcv", norm_final, embed_table, preferred_element_type=fl) / width_root
    )
    capped = LOGIT_CAP * jnp.tanh(logit_raw / LOGIT_CAP)
    exp_logit = jnp.exp(capped)
    onehot_f = onehot.astype(fl)
    exp_total, target_logit = lax.psum(
        (jnp.sum(exp_logit, axis=-1), jnp.sum(capped * onehot_f, axis=-1)), "mp"
    )
    nll = jnp.log(exp_total) - target_logit
    select = table_of_column[None, :, None] == jnp.arange(TABLES, dtype=jnp.int32)[None, None, :]
    counts = jnp.sum(jnp.where(select, fanout[:, None, :], 0), axis=-1).astype(fl)
    row_scale = 1.0 / (counts * row_total_count)
    ratio = capped / LOGIT_CAP
    d_logit = (
        (exp_logit / exp_total[:, :, None] - onehot_f)
        * row_scale[:, :, None]
        * (1.0 - ratio * ratio)
    ).astype(jnp.bfloat16)
    d_final_part = (
        jnp.einsum("rcv,cvd->rcd", d_logit, embed_table, preferred_element_type=fl) / width_root
    )
    table_grad = (
        jnp.einsum("rcv,rcd->cvd", d_logit, norm_final, preferred_element_type=fl) / width_root
    )
    d_final = lax.psum(d_final_part, "mp")
    back_full = norm_back_full(out_full, d_final, gain_final, rms_final)
    d_out_cols = lax.dynamic_slice_in_dim(back_full, mp_rank * part_width, part_width, 2).astype(
        jnp.bfloat16
    )
    d_out = cols_to_rows(d_out_cols)
    d_out_full = gather_features(d_out)
    d_hidden = jnp.einsum("rpd,df->rpf", d_out_full, w_down, preferred_element_type=fl)
    sigmoid_gate = jax.nn.sigmoid(gate_pre)
    d_gate = (d_hidden * up_proj * sigmoid_gate * (1.0 + gate_pre * (1.0 - sigmoid_gate))).astype(
        jnp.bfloat16
    )
    d_up = (d_hidden * gate_pre * sigmoid_gate).astype(jnp.bfloat16)
    d_norm_mlp = jnp.einsum("rpf,df->rpd", d_gate, w_gate, preferred_element_type=fl) + jnp.einsum(
        "rpf,df->rpd", d_up, w_up, preferred_element_type=fl
    )
    d_mid = (
        d_out.astype(fl)
        + norm_back_part(
            resid_mid, feature_sum(d_norm_mlp), own_part(gain_mlp), rms_mlp, model_width
        )
    ).astype(jnp.bfloat16)
    mid_grad_full = gather_features(d_mid)
    d_attn = jnp.einsum("rpd,dj->rpj", mid_grad_full, w_out, preferred_element_type=fl).astype(
        jnp.bfloat16
    )
    d_attn = d_attn.reshape(rows_here, col_count, local_heads, HS)
    d_prob = jnp.einsum("rqhe,rkhe->rhqk", d_attn, value_rows, preferred_element_type=fl)
    ratio_s = score / ATTN_CAP
    d_score = attn_prob * (d_prob - jnp.sum(attn_prob * d_prob, axis=-1, keepdims=True))
    d_scaled = (d_score * (1.0 - ratio_s * ratio_s) / math.sqrt(HS)).astype(jnp.bfloat16)
    d_query = jnp.einsum("rhqk,rkhe->rqhe", d_scaled, key_rows, preferred_element_type=fl)
    d_key = jnp.einsum("rhqk,rqhe->rkhe", d_scaled, queries, preferred_element_type=fl)
    d_value = jnp.einsum("rhqk,rqhe->rkhe", prob_b, d_attn, preferred_element_type=fl)
    d_qkv = (
        jnp.stack([d_query, d_key, d_value], axis=2)
        .reshape(rows_here, col_count, 3, head_cols)
        .astype(jnp.bfloat16)
    )
    d_norm_attn = jnp.einsum("rptx,dtx->rpd", d_qkv, w_qkv, preferred_element_type=fl)
    d_in = (
        d_mid.astype(fl)
        + norm_back_part(
            resid_in, feature_sum(d_norm_attn), own_part(gain_attn), rms_attn, model_width
        )
    ).astype(jnp.bfloat16)
    d_embed_rows = jnp.concatenate(
        [d_in[:, 1:], jnp.zeros((rows_here, 1, part_width), jnp.bfloat16)], axis=1
    )
    d_embed_cols = rows_to_cols(d_embed_rows)
    d_embed_full = gather_features(d_embed_cols)
    table_grad = table_grad + jnp.einsum(
        "rcv,rcd->cvd", onehot, d_embed_full, preferred_element_type=fl
    )
    qkv_term = jnp.einsum("rpd,rptx->dtx", norm_attn, d_qkv, preferred_element_type=fl).reshape(
        model_width, 3 * head_cols
    )
    out_term = jnp.einsum("rpd,rpj->dj", mid_grad_full, attn_out, preferred_element_type=fl)
    whole_terms = jnp.concatenate(
        [
            jnp.concatenate([qkv_term, out_term], axis=1),
            jnp.concatenate(
                [
                    jnp.einsum("rpd,rpf->df", norm_mlp, d_gate, preferred_element_type=fl),
                    jnp.einsum("rpd,rpf->df", norm_mlp, d_up, preferred_element_type=fl),
                    jnp.einsum("rpd,rpf->df", d_out_full, hidden, preferred_element_type=fl),
                ],
                axis=1,
            ),
        ],
        axis=1,
    )
    summed = lax.psum_scatter(whole_terms, "dp", scatter_dimension=0, tiled=True)
    ff_part = w_gate.shape[1]
    qkv_width = 3 * head_cols
    grad_qkv = summed[:, :qkv_width].reshape(summed.shape[0], 3, head_cols)
    grad_out = summed[:, qkv_width : qkv_width + head_cols]
    base = qkv_width + head_cols
    grad_gate = summed[:, base : base + ff_part]
    grad_up = summed[:, base + ff_part : base + 2 * ff_part]
    grad_down = summed[:, base + 2 * ff_part : base + 3 * ff_part]
    return (nll, table_grad, grad_qkv, grad_out, grad_gate, grad_up, grad_down)


def solution(mesh):
    return jax.shard_map(
        local,
        mesh=mesh,
        in_specs=(
            P(None, "dp"),
            P(),
            P("dp"),
            P("dp", "mp", None),
            P(),
            P(),
            P(),
            P(),
            P(None, None, "mp"),
            P(None, "mp"),
            P(None, "mp"),
            P(None, "mp"),
            P(None, "mp"),
        ),
        out_specs=(
            P(None, "dp"),
            P("dp", "mp", None),
            P("dp", None, "mp"),
            P("dp", "mp"),
            P("dp", "mp"),
            P("dp", "mp"),
            P("dp", "mp"),
        ),
        check_vma=False,
    )
```

profile of v0, /device:TPU:2, one launch (start us, length us, event | category | flops | bytes accessed | tf_op | source)
XLA Modules:
  0.0 726.3 jit_solution(7134462608592402723)
XLA Ops:
  8.0 2.4 convolution_bitcast_fusion
  10.4 44.1 %reduce-scatter.9.cloned.1.call-done = f32[128,2,128]{2,0,1:T(8,128)} async-done(((f32[128,2,1024]{2,0,1:T(8,128)}), f32[128,2,128]{2,0,1:T(8,128)}) %reduce-scatter.9.cloned.1.call-update) | async-done | bytes 131088 | tf_op jit(solution)/shard_map/reduce_scatter | solution.py:19
  56.1 10.0 %all-to-all-start = ((bf16[128,2,128]{2,1,0:T(2,128)(2,1)}), bf16[128,2,128]{2,1,0:T(2,128)(2,1)S(1)}, u32[]{:S(2)}, u32[]{:S(2)}) async-start(bf16[128,2,128]{2,1,0:T(2,128)(2,1)} %copy.114), calls=%async_computation.1 | async-start | bytes 131072 | tf_op jit(solution)/shard_map/all_to_all | solution.py:23
  67.7 8.4 %all-to-all-done = bf16[128,2,128]{2,1,0:T(2,128)(2,1)S(1)} async-done(((bf16[128,2,128]{2,1,0:T(2,128)(2,1)}), bf16[128,2,128]{2,1,0:T(2,128)(2,1)S(1)}, u32[]{:S(2)}, u32[]{:S(2)}) %all-to-all-start) | async-done | bytes 65568 | tf_op jit(solution)/shard_map/all_to_all | solution.py:23
  76.8 26.7 %all_gather.18 = bf16[4,64,1024]{2,1,0:T(8,128)(2,1)S(1)} all-gather(bf16[4,64,128]{2,1,0:T(8,128)(2,1)S(1)} %get-tuple-element.52), channel_id=1, replica_groups=mesh['dp'=32,'mp'=8] {'mp'}, dimensions={2}, use_global_device_ids=true | all-gather | bytes 589824 | tf_op jit(solution)/shard_map/all_gather | solution.py:15
  108.4 34.5 %reduce-scatter.11.cloned.1.call-done = f32[4,64,128]{2,1,0:T(8,128)} async-done(((f32[4,64,1024]{2,1,0:T(8,128)}), f32[4,64,128]{2,1,0:T(8,128)}) %reduce-scatter.11.cloned.1.call-update) | async-done | bytes 131088 | tf_op jit(solution)/shard_map/reduce_scatter | solution.py:19
  143.8 26.9 %all_gather.19 = bf16[4,64,1024]{2,1,0:T(8,128)(2,1)S(1)} all-gather(bf16[4,64,128]{2,1,0:T(8,128)(2,1)S(1)} %add_convert_fusion), channel_id=1, replica_groups=mesh['dp'=32,'mp'=8] {'mp'}, dimensions={2}, use_global_device_ids=true | all-gather | bytes 589824 | tf_op jit(solution)/shard_map/all_gather | solution.py:15
  174.1 2.5 multiply_convert_fusion.3
  178.3 40.9 %reduce-scatter.13.cloned.1.call-done = f32[4,64,128]{2,1,0:T(8,128)} async-done(((f32[4,64,1024]{2,1,0:T(8,128)}), f32[4,64,128]{2,1,0:T(8,128)}) %reduce-scatter.13.cloned.1.call-update) | async-done | bytes 131088 | tf_op jit(solution)/shard_map/reduce_scatter | solution.py:19
  220.9 10.0 %all-to-all-start.1 = ((bf16[4,64,128]{2,0,1:T(4,128)(2,1)}), bf16[4,64,128]{2,0,1:T(4,128)(2,1)S(1)}, u32[]{:S(2)}, u32[]{:S(2)}) async-start(bf16[4,64,128]{2,0,1:T(4,128)(2,1)} %copy.121), calls=%async_computation.4 | async-start | bytes 131072 | tf_op jit(solution)/shard_map/all_to_all | solution.py:27
  231.5 9.3 %all-to-all-done.1 = bf16[4,64,128]{2,0,1:T(4,128)(2,1)S(1)} async-done(((bf16[4,64,128]{2,0,1:T(4,128)(2,1)}), bf16[4,64,128]{2,0,1:T(4,128)(2,1)S(1)}, u32[]{:S(2)}, u32[]{:S(2)}) %all-to-all-start.1) | async-done | bytes 65568 | tf_op jit(solution)/shard_map/all_to_all | solution.py:27
  240.9 26.7 %all_gather.20 = bf16[128,2,1024]{2,0,1:T(8,128)(2,1)S(1)} all-gather(bf16[128,2,128]{2,0,1:T(8,128)(2,1)S(1)} %bitcast.144), channel_id=1, replica_groups=mesh['dp'=32,'mp'=8] {'mp'}, dimensions={2}, use_global_device_ids=true | all-gather | bytes 589824 | tf_op jit(solution)/shard_map/all_gather | solution.py:15
  269.9 14.4 %psum.35 = f32[128,2]{0,1:T(2,128)S(1)} all-reduce(f32[128,2]{0,1:T(2,128)} %get-tuple-element.35), channel_id=1, replica_groups=mesh['dp'=32,'mp'=8] {'mp'}, use_global_device_ids=true, to_apply=%region_8.9 | all-reduce | flops 256 | bytes 2048 | tf_op jit(solution)/shard_map/psum | solution.py:136
  287.8 76.1 %all-reduce.4.cloned.1.call-done = f32[128,2,1024]{2,0,1:T(8,128)} async-done(((f32[128,2,1024]{2,0,1:T(8,128)}), f32[128,2,1024]{2,0,1:T(8,128)}) %all-reduce.4.cloned.1.call-update) | async-done | bytes 1048592 | tf_op jit(solution)/shard_map/psum | solution.py:155
  366.6 19.4 %all_to_all.72 = bf16[128,2,128]{2,1,0:T(2,128)(2,1)S(1)} all-to-all(bf16[128,2,128]{2,1,0:T(2,128)(2,1)S(1)} %copy.124), channel_id=1, replica_groups=mesh['dp'=32,'mp'=8] {'dp'}, dimensions={0} | all-to-all | bytes 131072 | tf_op jit(solution)/shard_map/all_to_all | solution.py:23
  386.1 26.0 %all_gather.21 = bf16[4,64,1024]{2,1,0:T(8,128)(2,1)S(1)} all-gather(bf16[4,64,128]{2,1,0:T(8,128)(2,1)S(1)} %bitcast.138), channel_id=1, replica_groups=mesh['dp'=32,'mp'=8] {'mp'}, dimensions={2}, use_global_device_ids=true | all-gather | bytes 589824 | tf_op jit(solution)/shard_map/all_gather | solution.py:15
  417.6 33.3 %reduce-scatter.15.cloned.1.call-done = f32[4,64,128]{2,1,0:T(8,128)} async-done(((f32[4,64,1024]{2,1,0:T(8,128)}), f32[4,64,128]{2,1,0:T(8,128)}) %reduce-scatter.15.cloned.1.call-update) | async-done | bytes 131088 | tf_op jit(solution)/shard_map/reduce_scatter | solution.py:19
  452.5 18.0 %psum.38 = f32[4,64]{1,0:T(4,128)} all-reduce(f32[4,64]{1,0:T(4,128)} %fusion.46), channel_id=1, replica_groups=mesh['dp'=32,'mp'=8] {'mp'}, use_global_device_ids=true, to_apply=%region_16.17 | all-reduce | flops 256 | bytes 2048 | tf_op jit(solution)/shard_map/psum | solution.py:50
  472.2 27.0 %all_gather.22 = bf16[4,64,1024]{2,1,0:T(8,128)(2,1)S(1)} all-gather(bf16[4,64,128]{2,1,0:T(8,128)(2,1)S(1)} %fusion.61), channel_id=1, replica_groups=mesh['dp'=32,'mp'=8] {'mp'}, dimensions={2}, use_global_device_ids=true | all-gather | bytes 589824 | tf_op jit(solution)/shard_map/all_gather | solution.py:15
  506.3 2.2 convolution_convert_fusion.2
  510.7 2.6 convolution_bitcast_fusion.1
  513.6 2.7 bitcast_dynamic-update-slice_fusion.3
  518.2 2.8 bitcast_dynamic-update-slice_fusion.2
  521.1 2.6 bitcast_dynamic-update-slice_fusion.1
  525.4 9.2 %copy.156 = f32[1024,2048]{1,0:T(8,128)} copy(f32[1024,2048]{0,1:T(8,128)} %bitcast_dynamic-update-slice_fusion) | data formatting | bytes 16777216
  537.2 17.6 %reduce-scatter.17.cloned.1.call-done = f32[4,64,128]{2,1,0:T(8,128)} async-done(((f32[4,64,1024]{2,1,0:T(8,128)}), f32[4,64,128]{2,1,0:T(8,128)}) %reduce-scatter.17.cloned.1.call-update) | async-done | bytes 131088 | tf_op jit(solution)/shard_map/reduce_scatter | solution.py:19
  555.9 17.3 %all-reduce.1 = (f32[128,2]{0,1:T(2,128)S(1)}, f32[4,64]{1,0:T(4,128)S(1)}) all-reduce(f32[128,2]{0,1:T(2,128)S(1)} %copy-done.36, f32[4,64]{1,0:T(4,128)S(1)} %get-tuple-element.39), channel_id=1, replica_groups=mesh['dp'=32,'mp'=8] {'mp'}, use_global_device_ids=true, to_apply=%region_10.11 | all-reduce | flops 512 | bytes 4096 | tf_op jit(solution)/shard_map/psum | solution.py:136
  574.1 10.0 %all-to-all-start.3 = ((bf16[4,64,128]{2,0,1:T(4,128)(2,1)}), bf16[4,64,128]{2,0,1:T(4,128)(2,1)S(1)}, u32[]{:S(2)}, u32[]{:S(2)}) async-start(bf16[4,64,128]{2,0,1:T(4,128)(2,1)} %concatenate.12.clone), calls=%async_computation.8 | async-start | bytes 131072 | tf_op jit(solution)/shard_map/all_to_all | solution.py:27
  584.6 9.4 %all-to-all-done.3 = bf16[4,64,128]{2,0,1:T(4,128)(2,1)S(1)} async-done(((bf16[4,64,128]{2,0,1:T(4,128)(2,1)}), bf16[4,64,128]{2,0,1:T(4,128)(2,1)S(1)}, u32[]{:S(2)}, u32[]{:S(2)}) %all-to-all-start.3) | async-done | bytes 65568 | tf_op jit(solution)/shard_map/all_to_all | solution.py:27
  594.0 28.0 %all_gather.23 = bf16[128,2,1024]{2,0,1:T(8,128)(2,1)S(1)} all-gather(bf16[128,2,128]{2,0,1:T(8,128)(2,1)S(1)} %bitcast.145), channel_id=1, replica_groups=mesh['dp'=32,'mp'=8] {'mp'}, dimensions={2}, use_global_device_ids=true | all-gather | bytes 589824 | tf_op jit(solution)/shard_map/all_gather | solution.py:15
  622.0 2.5 convolution_add_fusion
  624.5 90.4 %reduce-scatter.19.cloned.1.call-done = f32[32,2048]{1,0:T(8,128)} async-done(((f32[1024,2048]{1,0:T(8,128)}), f32[32,2048]{1,0:T(8,128)}) %reduce-scatter.19.cloned.1.call-update) | async-done | bytes 262160
  (169 shorter events, 57.8 us)
Async XLA Ops:
  7.2 169.5 %copy-start = (bf16[1024,512]{1,0:T(8,128)(2,1)S(1)}, bf16[1024,512]{1,0:T(8,128)(2,1)}, u32[]{:S(2)}) copy-start(bf16[1024,512]{1,0:T(8,128)(2,1)} %param.25) | copy-start | bytes 3145732
  7.2 99.8 %copy-start.6 = (bf16[1024,128]{1,0:T(8,128)(2,1)S(1)}, bf16[1024,128]{1,0:T(8,128)(2,1)}, u32[]{:S(2)}) copy-start(bf16[1024,128]{1,0:T(8,128)(2,1)} %param.22) | copy-start | bytes 786436
  7.2 101.1 %copy-start.35 = (bf16[1024]{0:T(1024)(128)(2,1)S(1)}, bf16[1024]{0:T(1024)(128)(2,1)}, u32[]{:S(2)}) copy-start(bf16[1024]{0:T(1024)(128)(2,1)} %param.19) | copy-start | bytes 6148
  7.2 47.3 %reduce-scatter.9.cloned.1.call-start = ((), (), s32[]{:S(2)}) async-start(), calls=%async_computation.10 | async-start | bytes 1179648 | tf_op jit(solution)/shard_map/reduce_scatter | solution.py:19
  56.1 20.0 %all-to-all-start = ((bf16[128,2,128]{2,1,0:T(2,128)(2,1)}), bf16[128,2,128]{2,1,0:T(2,128)(2,1)S(1)}, u32[]{:S(2)}, u32[]{:S(2)}) async-start(bf16[128,2,128]{2,1,0:T(2,128)(2,1)} %copy.114), calls=%async_computation.1 | async-start | bytes 131072 | tf_op jit(solution)/shard_map/all_to_all | solution.py:23
  66.1 76.7 %reduce-scatter.11.cloned.1.call-start = ((), (), s32[]{:S(2)}) async-start(), calls=%async_computation.11 | async-start | bytes 1179648 | tf_op jit(solution)/shard_map/reduce_scatter | solution.py:19
  66.9 39.3 %copy-start.30 = (f32[1024]{0:T(1024)}, f32[1024]{0:T(1024)S(1)}, u32[]{:S(2)}) copy-start(f32[1024]{0:T(1024)S(1)} %convert_element_type.117) | copy-start | bytes 12292
  67.7 76.2 %copy-start.28 = (pred[64,64]{0,1:T(8,128)(4,1)}, pred[64,64]{0,1:T(8,128)(4,1)S(1)}, u32[]{:S(2)}) copy-start(pred[64,64]{0,1:T(8,128)(4,1)S(1)} %iota_compare_fusion.3) | copy-start | bytes 12292
  106.1 36.8 %copy-start.21 = (bf16[4,64,1,128]{1,3,0,2:T(8,128)(2,1)}, bf16[4,64,1,128]{1,3,0,2:T(8,128)(2,1)S(1)}, u32[]{:S(2)}) copy-start(bf16[4,64,1,128]{1,3,0,2:T(8,128)(2,1)S(1)} %copy.165) | copy-start | bytes 196612
  106.2 36.7 %copy-start.13 = (bf16[4,64,2,64]{3,2,1,0:T(2,128)(2,1)}, bf16[4,64,2,64]{3,2,1,0:T(2,128)(2,1)S(1)}, u32[]{:S(2)}) copy-start(bf16[4,64,2,64]{3,2,1,0:T(2,128)(2,1)S(1)} %reshape_squeeze.9) | copy-start | bytes 196612
  106.4 36.5 %copy-start.22 = (bf16[4,64,1,128]{1,3,0,2:T(8,128)(2,1)}, bf16[4,64,1,128]{1,3,0,2:T(8,128)(2,1)S(1)}, u32[]{:S(2)}) copy-start(bf16[4,64,1,128]{1,3,0,2:T(8,128)(2,1)S(1)} %copy.164) | copy-start | bytes 196612
  106.7 64.0 %copy-start.39 = (f32[4,2,64]{2,1,0:T(2,128)}, f32[4,2,64]{2,1,0:T(2,128)S(1)}, u32[]{:S(2)}) copy-start(f32[4,2,64]{2,1,0:T(2,128)S(1)} %get-tuple-element.59) | copy-start | bytes 6148
  106.9 35.9 %copy-start.14 = (bf16[4,2,64,64]{3,2,1,0:T(8,128)(2,1)}, bf16[4,2,64,64]{3,2,1,0:T(8,128)(2,1)S(1)}, u32[]{:S(2)}) copy-start(bf16[4,2,64,64]{3,2,1,0:T(8,128)(2,1)S(1)} %convolution_convert_fusion.4) | copy-start | bytes 196612
  108.3 111.0 %reduce-scatter.13.cloned.1.call-start = ((), (), s32[]{:S(2)}) async-start(), calls=%async_computation.12 | async-start | bytes 1179648 | tf_op jit(solution)/shard_map/reduce_scatter | solution.py:19
  108.4 69.7 %copy-start.31 = (f32[1024]{0:T(1024)}, f32[1024]{0:T(1024)S(1)}, u32[]{:S(2)}) copy-start(f32[1024]{0:T(1024)S(1)} %convert_element_type.126) | copy-start | bytes 12292
  171.5 96.8 %copy-start.1 = (bf16[2,128,1024]{2,1,0:T(8,128)(2,1)S(1)}, bf16[2,128,1024]{2,1,0:T(8,128)(2,1)}, u32[]{:S(2)}) copy-start(bf16[2,128,1024]{2,1,0:T(8,128)(2,1)} %param.16) | copy-start | bytes 1572868
  176.7 64.2 %copy-start.7 = (bf16[4,64,512]{2,1,0:T(8,128)(2,1)}, bf16[4,64,512]{2,1,0:T(8,128)(2,1)S(1)}, u32[]{:S(2)}) copy-start(bf16[4,64,512]{2,1,0:T(8,128)(2,1)S(1)} %get-tuple-element.61) | copy-start | bytes 786436
  220.9 20.0 %all-to-all-start.1 = ((bf16[4,64,128]{2,0,1:T(4,128)(2,1)}), bf16[4,64,128]{2,0,1:T(4,128)(2,1)S(1)}, u32[]{:S(2)}, u32[]{:S(2)}) async-start(bf16[4,64,128]{2,0,1:T(4,128)(2,1)} %copy.121), calls=%async_computation.4 | async-start | bytes 131072 | tf_op jit(solution)/shard_map/all_to_all | solution.py:27
  230.9 133.0 %all-reduce.4.cloned.1.call-start = ((), (), s32[]{:S(2)}) async-start(), calls=%async_computation.13 | async-start | bytes 2097152 | tf_op jit(solution)/shard_map/psum | solution.py:155
  286.6 164.3 %reduce-scatter.15.cloned.1.call-start = ((), (), s32[]{:S(2)}) async-start(), calls=%async_computation.14 | async-start | bytes 1179648 | tf_op jit(solution)/shard_map/reduce_scatter | solution.py:19
  363.9 50.2 %copy-start.4 = (bf16[1024,512]{1,0:T(8,128)(2,1)S(1)}, bf16[1024,512]{1,0:T(8,128)(2,1)}, u32[]{:S(2)}) copy-start(bf16[1024,512]{1,0:T(8,128)(2,1)} %param.23) | copy-start | bytes 3145732
  363.9 51.0 %copy-start.5 = (bf16[1024,512]{1,0:T(8,128)(2,1)S(1)}, bf16[1024,512]{1,0:T(8,128)(2,1)}, u32[]{:S(2)}) copy-start(bf16[1024,512]{1,0:T(8,128)(2,1)} %param.24) | copy-start | bytes 3145732
  386.0 28.0 %copy-start.11 = (bf16[32,4,2,128]{3,2,0,1:T(2,128)(2,1)}, bf16[32,4,2,128]{3,2,0,1:T(2,128)(2,1)S(1)}, u32[]{:S(2)}) copy-start(bf16[32,4,2,128]{3,2,0,1:T(2,128)(2,1)S(1)} %copy.125) | copy-start | bytes 196612
  412.1 58.4 %copy-start.2 = (bf16[4,64,1024]{2,1,0:T(8,128)(2,1)}, bf16[4,64,1024]{2,1,0:T(8,128)(2,1)S(1)}, u32[]{:S(2)}) copy-start(bf16[4,64,1024]{2,1,0:T(8,128)(2,1)S(1)} %all_gather.21) | copy-start | bytes 1572868
  416.3 138.5 %reduce-scatter.17.cloned.1.call-start = ((), (), s32[]{:S(2)}) async-start(), calls=%async_computation.15 | async-start | bytes 1179648 | tf_op jit(solution)/shard_map/reduce_scatter | solution.py:19
  513.3 10.3 %copy-start.8 = (bf16[4,64,512]{2,1,0:T(8,128)(2,1)S(1)}, bf16[4,64,512]{2,1,0:T(8,128)(2,1)}, u32[]{:S(2)}) copy-start(bf16[4,64,512]{2,1,0:T(8,128)(2,1)} %copy-done.7) | copy-start | bytes 786436
  513.3 201.6 %reduce-scatter.19.cloned.1.call-start = ((), (), s32[]{:S(2)}) async-start(), calls=%async_computation.16 | async-start | bytes 8650752
  513.6 10.1 %copy-start.3 = (bf16[4,64,1024]{2,1,0:T(8,128)(2,1)S(1)}, bf16[4,64,1024]{2,1,0:T(8,128)(2,1)}, u32[]{:S(2)}) copy-start(bf16[4,64,1024]{2,1,0:T(8,128)(2,1)} %copy-done.2) | copy-start | bytes 1572868
  534.7 21.2 %copy-start.36 = (f32[128,2]{0,1:T(2,128)S(1)}, f32[128,2]{0,1:T(2,128)}, u32[]{:S(2)}) copy-start(f32[128,2]{0,1:T(2,128)} %get-tuple-element.36) | copy-start | bytes 3076
  534.7 38.5 %copy-start.10 = (bf16[4,64,128]{2,1,0:T(8,128)(2,1)S(1)}, bf16[4,64,128]{2,1,0:T(8,128)(2,1)}, u32[]{:S(2)}) copy-start(bf16[4,64,128]{2,1,0:T(8,128)(2,1)} %copy-done.9) | copy-start | bytes 196612
  534.7 38.5 %copy-start.12 = (f32[4,64,128]{2,1,0:T(8,128)S(1)}, f32[4,64,128]{2,1,0:T(8,128)}, u32[]{:S(2)}) copy-start(f32[4,64,128]{2,1,0:T(8,128)} %get-tuple-element.51) | copy-start | bytes 393220
  574.1 19.9 %all-to-all-start.3 = ((bf16[4,64,128]{2,0,1:T(4,128)(2,1)}), bf16[4,64,128]{2,0,1:T(4,128)(2,1)S(1)}, u32[]{:S(2)}, u32[]{:S(2)}) async-start(bf16[4,64,128]{2,0,1:T(4,128)(2,1)} %concatenate.12.clone), calls=%async_computation.8 | async-start | bytes 131072 | tf_op jit(solution)/shard_map/all_to_all | solution.py:27
  (19 other events, 52.8 us)
Sparse Core Ops, SparseCore 0:
  11.1 43.3 reduce-scatter.8
  108.4 34.4 reduce-scatter.10
  178.3 40.9 reduce-scatter.12
  286.7 77.0 all-reduce.3
  416.4 34.4 reduce-scatter.14
  513.4 41.3 reduce-scatter.16
  559.2 155.6 reduce-scatter.18
where the time goes:
time: 728 us; the launch traced here: 726 us
  waiting for transfers between devices  364 us (50%)
  blocking collectives  230 us (32%)
  matrix products  46 us (6%)
  starting transfers between devices  30.4 us (4%)
  local copies, waits for them, and re-layouts  22.4 us (3%)
  other arithmetic  18.3 us (3%)
  between operations  14.7 us (2%)
    reduce_scatter x5, waiting for transfers between devices, feature_sum(): return lax.psum_scatter(term, 'mp', scatter_dimension=2, tiled=True)  170 us
    all_gather x6, blocking collectives, gather_features(): return lax.all_gather(values, 'mp', axis=2, tiled=True)  161 us
    unnamed x8, waiting for transfers between devices  90.5 us
    psum x1, waiting for transfers between devices, local(): d_final = lax.psum(d_final_part, 'mp')  76.1 us
    psum x2, blocking collectives, local(): lax.psum((jnp.sum(exp_logit, axis=-1), jnp.sum(capped * onehot_f, axis=-1...  31.7 us
    all_to_all x2, starting transfers between devices, rows_to_cols(): return lax.all_to_all(values, 'dp', split_axis=1, concat_axis=0, tiled=True)  20 us
    all_to_all x1, blocking collectives, cols_to_rows(): return lax.all_to_all(values, 'dp', split_axis=0, concat_axis=1, tiled=True)  19.4 us
    all_to_all x2, waiting for transfers between devices, rows_to_cols(): return lax.all_to_all(values, 'dp', split_axis=1, concat_axis=0, tiled=True)  18.7 us
  transfers between devices with their start and end apart: 10, of which 10 were waited for; matrix products, arithmetic and copies ran while one was open for 5% of the time, Pallas kernels for 0%

commit v1 on v0

--- a/solution.py
+++ b/solution.py
@@ -12,7 +12,9 @@
 
 
 def gather_features(values):
-    return lax.all_gather(values, "mp", axis=2, tiled=True)
+    return jnp.concatenate(
+        lax.all_to_all(jnp.stack([values] * lax.axis_size("mp")), "mp", 0, 0), axis=2
+    )
 
 
 def feature_sum(term):

time: 728 us -> 667 us (0.916)
  blocking collectives: 230 us -> 115 us
  waiting for transfers between devices: 364 us -> 401 us
  starting transfers between devices: 30.4 us -> 43.8 us
    all_gather x6 -> x0, blocking collectives: 161 us -> none  [gather_features(): return lax.all_gather(values, 'mp', axis=2, tiled=True)]
    all_to_all x0 -> x3, blocking collectives: none -> 44.3 us  [the longest x2 24.6 us: gather_features(): lax.all_to_all(jnp.stack([values] * lax.axis_size('mp')), 'mp', 0, 0)]
    all_to_all x0 -> x4, waiting for transfers between devices: none -> 29.3 us  [gather_features(): lax.all_to_all(jnp.stack([values] * lax.axis_size('mp')), 'mp', 0, 0)]
    all_to_all x0 -> x4, starting transfers between devices: none -> 23.6 us  [gather_features(): lax.all_to_all(jnp.stack([values] * lax.axis_size('mp')), 'mp', 0, 0)]
    unnamed x8, waiting for transfers between devices: 90.5 us -> 105 us
    all_to_all x2 -> x1, starting transfers between devices: 20 us -> 9.89 us  [rows_to_cols(): return lax.all_to_all(values, 'dp', split_axis=1, concat_axis=0, tiled=True)]
    all_to_all x2 -> x1, waiting for transfers between devices: 18.7 us -> 9.92 us  [rows_to_cols(): return lax.all_to_all(values, 'dp', split_axis=1, concat_axis=0, tiled=True)]
  transfers between devices with their start and end apart: 10 -> 13, of which waited for: 10 -> 13; matrix products, arithmetic and copies ran while one was open for 5% -> 5% of each run, Pallas kernels for 0% -> 0%
where the time goes in v1:
time: 667 us; the launch traced here: 665 us
  waiting for transfers between devices  401 us (60%)
  blocking collectives  115 us (17%)
  matrix products  45.7 us (7%)
  starting transfers between devices  43.8 us (7%)
  local copies, waits for them, and re-layouts  27.4 us (4%)
  other arithmetic  17.9 us (3%)
  between operations  14.6 us (2%)
    reduce_scatter x5, waiting for transfers between devices, feature_sum(): return lax.psum_scatter(term, 'mp', scatter_dimension=2, tiled=True)  173 us
    unnamed x8, waiting for transfers between devices  105 us
    psum x1, waiting for transfers between devices, local(): d_final = lax.psum(d_final_part, 'mp')  74.7 us
    psum x2, blocking collectives, local(): lax.psum((jnp.sum(exp_logit, axis=-1), jnp.sum(capped * onehot_f, axis=-1...  34.1 us
    all_to_all x4, waiting for transfers between devices, gather_features(): lax.all_to_all(jnp.stack([values] * lax.axis_size('mp')), 'mp', 0, 0)  29.3 us
    all_to_all x2, blocking collectives, gather_features(): lax.all_to_all(jnp.stack([values] * lax.axis_size('mp')), 'mp', 0, 0)  24.6 us
    all_to_all x4, starting transfers between devices, gather_features(): lax.all_to_all(jnp.stack([values] * lax.axis_size('mp')), 'mp', 0, 0)  23.6 us
    all_to_all x1, blocking collectives, rows_to_cols(): return lax.all_to_all(values, 'dp', split_axis=1, concat_axis=0, tiled=True)  19.6 us
  transfers between devices with their start and end apart: 13, of which 13 were waited for; matrix products, arithmetic and copies ran while one was open for 5% of the time, Pallas kernels for 0%

profile of v1, /device:TPU:2, one launch (start us, length us, event | category | flops | bytes accessed | tf_op | source)
XLA Modules:
  0.0 665.4 jit_solution(14718293753321374986)
XLA Ops:
  10.4 44.1 %reduce-scatter.9.cloned.1.call-done = f32[128,2,128]{2,0,1:T(8,128)} async-done(((f32[128,2,1024]{2,0,1:T(8,128)}), f32[128,2,128]{2,0,1:T(8,128)}) %reduce-scatter.9.cloned.1.call-update) | async-done | bytes 131088 | tf_op jit(solution)/shard_map/reduce_scatter | solution.py:21
  56.1 10.0 %all-to-all-start = ((bf16[128,2,128]{2,1,0:T(2,128)(2,1)}), bf16[128,2,128]{2,1,0:T(2,128)(2,1)S(1)}, u32[]{:S(2)}, u32[]{:S(2)}) async-start(bf16[128,2,128]{2,1,0:T(2,128)(2,1)} %copy.156), calls=%async_computation.1 | async-start | bytes 131072 | tf_op jit(solution)/shard_map/all_to_all | solution.py:25
  66.9 9.2 %all-to-all-done = bf16[128,2,128]{2,1,0:T(2,128)(2,1)S(1)} async-done(((bf16[128,2,128]{2,1,0:T(2,128)(2,1)}), bf16[128,2,128]{2,1,0:T(2,128)(2,1)S(1)}, u32[]{:S(2)}, u32[]{:S(2)}) %all-to-all-start) | async-done | bytes 65568 | tf_op jit(solution)/shard_map/all_to_all | solution.py:25
  77.7 5.7 all-to-all-start.1
  84.2 7.9 %all-to-all-done.1 = bf16[8,4,64,128]{3,2,1,0:T(8,128)(2,1)S(1)} async-done(((bf16[8,4,64,128]{3,2,1,0:T(8,128)(2,1)}), bf16[8,4,64,128]{3,2,1,0:T(8,128)(2,1)S(1)}, u32[]{:S(2)}, u32[]{:S(2)}) %all-to-all-start.1) | async-done | bytes 524320 | tf_op jit(solution)/shard_map/all_to_all | solution.py:16
  96.8 34.7 %reduce-scatter.11.cloned.1.call-done = f32[4,64,128]{2,1,0:T(8,128)} async-done(((f32[4,64,1024]{2,1,0:T(8,128)}), f32[4,64,128]{2,1,0:T(8,128)}) %reduce-scatter.11.cloned.1.call-update) | async-done | bytes 131088 | tf_op jit(solution)/shard_map/reduce_scatter | solution.py:21
  133.3 6.1 all-to-all-start.2
  139.4 6.7 %all-to-all-done.2 = bf16[8,4,64,128]{3,2,1,0:T(8,128)(2,1)S(1)} async-done(((bf16[8,4,64,128]{3,2,1,0:T(8,128)(2,1)}), bf16[8,4,64,128]{3,2,1,0:T(8,128)(2,1)S(1)}, u32[]{:S(2)}, u32[]{:S(2)}) %all-to-all-start.2) | async-done | bytes 524320 | tf_op jit(solution)/shard_map/all_to_all | solution.py:16
  148.6 2.7 multiply_convert_fusion.3
  152.9 41.0 %reduce-scatter.13.cloned.1.call-done = f32[4,64,128]{2,1,0:T(8,128)} async-done(((f32[4,64,1024]{2,1,0:T(8,128)}), f32[4,64,128]{2,1,0:T(8,128)}) %reduce-scatter.13.cloned.1.call-update) | async-done | bytes 131088 | tf_op jit(solution)/shard_map/reduce_scatter | solution.py:21
  195.5 9.9 %all-to-all-start.3 = ((bf16[4,64,128]{2,0,1:T(4,128)(2,1)}), bf16[4,64,128]{2,0,1:T(4,128)(2,1)S(1)}, u32[]{:S(2)}, u32[]{:S(2)}) async-start(bf16[4,64,128]{2,0,1:T(4,128)(2,1)} %copy.165), calls=%async_computation.6 | async-start | bytes 131072 | tf_op jit(solution)/shard_map/all_to_all | solution.py:29
  205.4 9.9 %all-to-all-done.3 = bf16[4,64,128]{2,0,1:T(4,128)(2,1)S(1)} async-done(((bf16[4,64,128]{2,0,1:T(4,128)(2,1)}), bf16[4,64,128]{2,0,1:T(4,128)(2,1)S(1)}, u32[]{:S(2)}, u32[]{:S(2)}) %all-to-all-start.3) | async-done | bytes 65568 | tf_op jit(solution)/shard_map/all_to_all | solution.py:29
  216.3 5.8 all-to-all-start.4
  223.4 7.2 %all-to-all-done.4 = bf16[8,128,2,128]{3,1,2,0:T(8,128)(2,1)S(1)} async-done(((bf16[8,128,2,128]{3,1,2,0:T(8,128)(2,1)}), bf16[8,128,2,128]{3,1,2,0:T(8,128)(2,1)S(1)}, u32[]{:S(2)}, u32[]{:S(2)}) %all-to-all-start.4) | async-done | bytes 524320 | tf_op jit(solution)/shard_map/all_to_all | solution.py:16
  233.0 16.9 %psum.35 = f32[128,2]{0,1:T(2,128)S(1)} all-reduce(f32[128,2]{0,1:T(2,128)} %get-tuple-element.42), channel_id=1, replica_groups=mesh['dp'=32,'mp'=8] {'mp'}, use_global_device_ids=true, to_apply=%region_8.9 | all-reduce | flops 256 | bytes 2048 | tf_op jit(solution)/shard_map/psum | solution.py:138
  253.3 74.7 %all-reduce.4.cloned.1.call-done = f32[128,2,1024]{2,0,1:T(8,128)} async-done(((f32[128,2,1024]{2,0,1:T(8,128)}), f32[128,2,1024]{2,0,1:T(8,128)}) %all-reduce.4.cloned.1.call-update) | async-done | bytes 1048592 | tf_op jit(solution)/shard_map/psum | solution.py:157
  330.8 19.4 %all_to_all.96 = bf16[128,2,128]{2,1,0:T(2,128)(2,1)S(1)} all-to-all(bf16[128,2,128]{2,1,0:T(2,128)(2,1)S(1)} %copy.169), channel_id=1, replica_groups=mesh['dp'=32,'mp'=8] {'dp'}, dimensions={0} | all-to-all | bytes 131072 | tf_op jit(solution)/shard_map/all_to_all | solution.py:25
  350.3 12.9 %all_to_all.97 = bf16[8,4,64,128]{3,2,1,0:T(8,128)(2,1)S(1)} all-to-all(bf16[8,4,64,128]{3,2,1,0:T(8,128)(2,1)S(1)} %stack.28), channel_id=1, replica_groups=mesh['dp'=32,'mp'=8] {'mp'}, dimensions={0} | all-to-all | bytes 1048576 | tf_op jit(solution)/shard_map/all_to_all | solution.py:16
  368.2 34.0 %reduce-scatter.15.cloned.1.call-done = f32[4,64,128]{2,1,0:T(8,128)} async-done(((f32[4,64,1024]{2,1,0:T(8,128)}), f32[4,64,128]{2,1,0:T(8,128)}) %reduce-scatter.15.cloned.1.call-update) | async-done | bytes 131088 | tf_op jit(solution)/shard_map/reduce_scatter | solution.py:21
  403.2 17.1 %psum.38 = f32[4,64]{1,0:T(4,128)S(1)} all-reduce(f32[4,64]{1,0:T(4,128)S(1)} %fusion.57), channel_id=1, replica_groups=mesh['dp'=32,'mp'=8] {'mp'}, use_global_device_ids=true, to_apply=%region_16.17 | all-reduce | flops 256 | bytes 2048 | tf_op jit(solution)/shard_map/psum | solution.py:52
  421.5 11.7 %all_to_all.98 = bf16[8,4,64,128]{3,2,1,0:T(8,128)(2,1)S(1)} all-to-all(bf16[8,4,64,128]{3,2,1,0:T(8,128)(2,1)S(1)} %stack.29), channel_id=1, replica_groups=mesh['dp'=32,'mp'=8] {'mp'}, dimensions={0} | all-to-all | bytes 1048576 | tf_op jit(solution)/shard_map/all_to_all | solution.py:16
  449.8 2.7 convolution_bitcast_fusion.1
  452.7 2.7 bitcast_dynamic-update-slice_fusion.3
  457.4 2.8 bitcast_dynamic-update-slice_fusion.2
  460.3 2.6 bitcast_dynamic-update-slice_fusion.1
  464.7 9.2 %copy.204 = f32[1024,2048]{1,0:T(8,128)} copy(f32[1024,2048]{0,1:T(8,128)} %bitcast_dynamic-update-slice_fusion) | data formatting | bytes 16777216
  474.9 19.2 %reduce-scatter.17.cloned.1.call-done = f32[4,64,128]{2,1,0:T(8,128)} async-done(((f32[4,64,1024]{2,1,0:T(8,128)}), f32[4,64,128]{2,1,0:T(8,128)}) %reduce-scatter.17.cloned.1.call-update) | async-done | bytes 131088 | tf_op jit(solution)/shard_map/reduce_scatter | solution.py:21
  495.2 17.2 %all-reduce.1 = (f32[128,2]{0,1:T(2,128)S(1)}, f32[4,64]{1,0:T(4,128)S(1)}) all-reduce(f32[128,2]{0,1:T(2,128)S(1)} %copy-done.30, f32[4,64]{1,0:T(4,128)S(1)} %get-tuple-element.46), channel_id=1, replica_groups=mesh['dp'=32,'mp'=8] {'mp'}, use_global_device_ids=true, to_apply=%region_10.11 | all-reduce | flops 512 | bytes 4096 | tf_op jit(solution)/shard_map/psum | solution.py:138
  512.8 19.6 %all_to_all.99 = bf16[4,64,128]{2,0,1:T(4,128)(2,1)S(1)} all-to-all(bf16[4,64,128]{2,0,1:T(4,128)(2,1)S(1)} %concatenate.12.clone), channel_id=1, replica_groups=mesh['dp'=32,'mp'=8] {'dp'}, dimensions={1} | all-to-all | bytes 131072 | tf_op jit(solution)/shard_map/all_to_all | solution.py:29
  533.3 6.1 all-to-all-start.9
  540.4 7.6 %all-to-all-done.9 = bf16[8,128,2,128]{3,1,2,0:T(8,128)(2,1)S(1)} async-done(((bf16[8,128,2,128]{3,1,2,0:T(8,128)(2,1)}), bf16[8,128,2,128]{3,1,2,0:T(8,128)(2,1)S(1)}, u32[]{:S(2)}, u32[]{:S(2)}) %all-to-all-start.9) | async-done | bytes 524320 | tf_op jit(solution)/shard_map/all_to_all | solution.py:16
  549.2 104.7 %reduce-scatter.19.cloned.1.call-done = f32[32,2048]{1,0:T(8,128)} async-done(((f32[1024,2048]{1,0:T(8,128)}), f32[32,2048]{1,0:T(8,128)}) %reduce-scatter.19.cloned.1.call-update) | async-done | bytes 262160
  (166 shorter events, 68.8 us)
Async XLA Ops:
  7.2 144.2 %copy-start = (bf16[1024,512]{1,0:T(8,128)(2,1)S(1)}, bf16[1024,512]{1,0:T(8,128)(2,1)}, u32[]{:S(2)}) copy-start(bf16[1024,512]{1,0:T(8,128)(2,1)} %param.25) | copy-start | bytes 3145732
  7.2 88.3 %copy-start.10 = (bf16[1024,128]{1,0:T(8,128)(2,1)S(1)}, bf16[1024,128]{1,0:T(8,128)(2,1)}, u32[]{:S(2)}) copy-start(bf16[1024,128]{1,0:T(8,128)(2,1)} %param.22) | copy-start | bytes 786436
  7.2 47.3 %reduce-scatter.9.cloned.1.call-start = ((), (), s32[]{:S(2)}) async-start(), calls=%async_computation.16 | async-start | bytes 1179648 | tf_op jit(solution)/shard_map/reduce_scatter | solution.py:21
  10.4 129.0 %copy-start.29 = (bf16[1024]{0:T(1024)(128)(2,1)S(1)}, bf16[1024]{0:T(1024)(128)(2,1)}, u32[]{:S(2)}) copy-start(bf16[1024]{0:T(1024)(128)(2,1)} %param.19) | copy-start | bytes 6148
  56.1 20.0 %all-to-all-start = ((bf16[128,2,128]{2,1,0:T(2,128)(2,1)}), bf16[128,2,128]{2,1,0:T(2,128)(2,1)S(1)}, u32[]{:S(2)}, u32[]{:S(2)}) async-start(bf16[128,2,128]{2,1,0:T(2,128)(2,1)} %copy.156), calls=%async_computation.1 | async-start | bytes 131072 | tf_op jit(solution)/shard_map/all_to_all | solution.py:25
  77.7 14.3 %all-to-all-start.1 = ((bf16[8,4,64,128]{3,2,1,0:T(8,128)(2,1)}), bf16[8,4,64,128]{3,2,1,0:T(8,128)(2,1)S(1)}, u32[]{:S(2)}, u32[]{:S(2)}) async-start(bf16[8,4,64,128]{3,2,1,0:T(8,128)(2,1)} %stack.24), calls=%async_computation.2 | async-start | bytes 1048576 | tf_op jit(solution)/shard_map/all_to_all | solution.py:16
  83.4 48.0 %reduce-scatter.11.cloned.1.call-start = ((), (), s32[]{:S(2)}) async-start(), calls=%async_computation.17 | async-start | bytes 1179648 | tf_op jit(solution)/shard_map/reduce_scatter | solution.py:21
  84.1 62.7 %copy-start.24 = (f32[1024]{0:T(1024)}, f32[1024]{0:T(1024)S(1)}, u32[]{:S(2)}) copy-start(f32[1024]{0:T(1024)S(1)} %convert_element_type.150) | copy-start | bytes 12292
  84.1 62.7 %copy-start.22 = (pred[64,64]{0,1:T(8,128)(4,1)}, pred[64,64]{0,1:T(8,128)(4,1)S(1)}, u32[]{:S(2)}) copy-start(pred[64,64]{0,1:T(8,128)(4,1)S(1)} %iota_compare_fusion.3) | copy-start | bytes 12292
  92.8 54.0 %copy-start.20 = (f32[4,64]{1,0:T(4,128)}, f32[4,64]{1,0:T(4,128)S(1)}, u32[]{:S(2)}) copy-start(f32[4,64]{1,0:T(4,128)S(1)} %get-tuple-element.61) | copy-start | bytes 3076
  94.6 38.7 %copy-start.14 = (bf16[4,64,1,128]{1,3,0,2:T(8,128)(2,1)}, bf16[4,64,1,128]{1,3,0,2:T(8,128)(2,1)S(1)}, u32[]{:S(2)}) copy-start(bf16[4,64,1,128]{1,3,0,2:T(8,128)(2,1)S(1)} %copy.213) | copy-start | bytes 196612
  94.7 56.6 %copy-start.7 = (bf16[4,64,2,64]{3,2,1,0:T(2,128)(2,1)}, bf16[4,64,2,64]{3,2,1,0:T(2,128)(2,1)S(1)}, u32[]{:S(2)}) copy-start(bf16[4,64,2,64]{3,2,1,0:T(2,128)(2,1)S(1)} %reshape_squeeze.9) | copy-start | bytes 196612
  95.2 50.9 %copy-start.33 = (f32[4,2,64]{2,1,0:T(2,128)}, f32[4,2,64]{2,1,0:T(2,128)S(1)}, u32[]{:S(2)}) copy-start(f32[4,2,64]{2,1,0:T(2,128)S(1)} %get-tuple-element.66) | copy-start | bytes 6148
  95.5 55.9 %copy-start.8 = (bf16[4,2,64,64]{3,2,1,0:T(8,128)(2,1)}, bf16[4,2,64,64]{3,2,1,0:T(8,128)(2,1)S(1)}, u32[]{:S(2)}) copy-start(bf16[4,2,64,64]{3,2,1,0:T(8,128)(2,1)S(1)} %convolution_convert_fusion.4) | copy-start | bytes 196612
  133.3 12.8 %all-to-all-start.2 = ((bf16[8,4,64,128]{3,2,1,0:T(8,128)(2,1)}), bf16[8,4,64,128]{3,2,1,0:T(8,128)(2,1)S(1)}, u32[]{:S(2)}, u32[]{:S(2)}) async-start(bf16[8,4,64,128]{3,2,1,0:T(8,128)(2,1)} %stack.25), calls=%async_computation.4 | async-start | bytes 1048576 | tf_op jit(solution)/shard_map/all_to_all | solution.py:16
  139.4 54.5 %reduce-scatter.13.cloned.1.call-start = ((), (), s32[]{:S(2)}) async-start(), calls=%async_computation.18 | async-start | bytes 1179648 | tf_op jit(solution)/shard_map/reduce_scatter | solution.py:21
  146.9 58.5 %copy-start.28 = (bf16[1024]{0:T(1024)(128)(2,1)S(1)}, bf16[1024]{0:T(1024)(128)(2,1)}, u32[]{:S(2)}) copy-start(bf16[1024]{0:T(1024)(128)(2,1)} %param.20) | copy-start | bytes 6148
  146.9 75.1 %copy-start.31 = (s32[2]{0:T(128)S(1)}, s32[2]{0:T(128)}, u32[]{:S(2)}) copy-start(s32[2]{0:T(128)} %param.15) | copy-start | bytes 28
  148.6 82.8 %copy-start.1 = (bf16[2,128,1024]{2,1,0:T(8,128)(2,1)S(1)}, bf16[2,128,1024]{2,1,0:T(8,128)(2,1)}, u32[]{:S(2)}) copy-start(bf16[2,128,1024]{2,1,0:T(8,128)(2,1)} %param.16) | copy-start | bytes 1572868
  195.5 19.8 %all-to-all-start.3 = ((bf16[4,64,128]{2,0,1:T(4,128)(2,1)}), bf16[4,64,128]{2,0,1:T(4,128)(2,1)S(1)}, u32[]{:S(2)}, u32[]{:S(2)}) async-start(bf16[4,64,128]{2,0,1:T(4,128)(2,1)} %copy.165), calls=%async_computation.6 | async-start | bytes 131072 | tf_op jit(solution)/shard_map/all_to_all | solution.py:29
  216.3 14.4 %all-to-all-start.4 = ((bf16[8,128,2,128]{3,1,2,0:T(8,128)(2,1)}), bf16[8,128,2,128]{3,1,2,0:T(8,128)(2,1)S(1)}, u32[]{:S(2)}, u32[]{:S(2)}) async-start(bf16[8,128,2,128]{3,1,2,0:T(8,128)(2,1)} %stack.27), calls=%async_computation.7 | async-start | bytes 1048576 | tf_op jit(solution)/shard_map/all_to_all | solution.py:16
  222.0 106.0 %all-reduce.4.cloned.1.call-start = ((), (), s32[]{:S(2)}) async-start(), calls=%async_computation.19 | async-start | bytes 2097152 | tf_op jit(solution)/shard_map/psum | solution.py:157
  252.2 150.0 %reduce-scatter.15.cloned.1.call-start = ((), (), s32[]{:S(2)}) async-start(), calls=%async_computation.20 | async-start | bytes 1179648 | tf_op jit(solution)/shard_map/reduce_scatter | solution.py:21
  253.3 167.0 %copy-start.17 = (f32[4,64]{1,0:T(4,128)S(1)}, f32[4,64]{1,0:T(4,128)}, u32[]{:S(2)}) copy-start(f32[4,64]{1,0:T(4,128)} %copy-done.16) | copy-start | bytes 3076
  253.3 167.0 %copy-start.18 = (f32[4,64]{1,0:T(4,128)S(1)}, f32[4,64]{1,0:T(4,128)}, u32[]{:S(2)}) copy-start(f32[4,64]{1,0:T(4,128)} %get-tuple-element.62) | copy-start | bytes 3076
  365.2 56.2 %copy-start.9 = (bf16[4,64,512]{2,1,0:T(8,128)(2,1)}, bf16[4,64,512]{2,1,0:T(8,128)(2,1)S(1)}, u32[]{:S(2)}) copy-start(bf16[4,64,512]{2,1,0:T(8,128)(2,1)S(1)} %get-tuple-element.51) | copy-start | bytes 786436
  367.4 126.8 %reduce-scatter.17.cloned.1.call-start = ((), (), s32[]{:S(2)}) async-start(), calls=%async_computation.21 | async-start | bytes 1179648 | tf_op jit(solution)/shard_map/reduce_scatter | solution.py:21
  452.5 201.5 %reduce-scatter.19.cloned.1.call-start = ((), (), s32[]{:S(2)}) async-start(), calls=%async_computation.22 | async-start | bytes 8650752
  473.9 65.5 %copy-start.13 = (f32[2,128,128]{1,2,0:T(8,128)S(1)}, f32[2,128,128]{1,2,0:T(8,128)}, u32[]{:S(2)}) copy-start(f32[2,128,128]{1,2,0:T(8,128)} %get-tuple-element.70) | copy-start | bytes 393220
  473.9 65.5 %copy-start.23 = (f32[128,2]{0,1:T(2,128)S(1)}, f32[128,2]{0,1:T(2,128)}, u32[]{:S(2)}) copy-start(f32[128,2]{0,1:T(2,128)} %multiply_divide_fusion) | copy-start | bytes 3076
  473.9 65.5 %copy-start.27 = (f32[128,2]{0,1:T(2,128)S(1)}, f32[128,2]{0,1:T(2,128)}, u32[]{:S(2)}) copy-start(f32[128,2]{0,1:T(2,128)} %copy-done.26) | copy-start | bytes 3076
  533.3 14.7 %all-to-all-start.9 = ((bf16[8,128,2,128]{3,1,2,0:T(8,128)(2,1)}), bf16[8,128,2,128]{3,1,2,0:T(8,128)(2,1)S(1)}, u32[]{:S(2)}, u32[]{:S(2)}) async-start(bf16[8,128,2,128]{3,1,2,0:T(8,128)(2,1)} %stack.35), calls=%async_computation.14 | async-start | bytes 1048576 | tf_op jit(solution)/shard_map/all_to_all | solution.py:16
  (16 other events, 257.7 us)
Sparse Core Ops, SparseCore 0:
  11.1 43.3 reduce-scatter.8
  96.9 34.4 reduce-scatter.10
  153.0 40.8 reduce-scatter.12
  252.3 75.6 all-reduce.3
  367.5 34.5 reduce-scatter.14
  452.6 41.4 reduce-scatter.16
  498.5 155.3 reduce-scatter.18
